TPU v7x, 32 devices: a whole 2x2x4 slice. The times are simulated.
32 devices in a mesh: groups: 2 (over x), face: 8 (over z, y), sub: 2 (over core).
Axes of the slice: x: 2, y: 2, z: 4, core: 2. Of those that a mesh axis runs over, the one named last changes fastest.
Arguments:
- features: bfloat16 [65536, 64], P(('groups', 'face', 'sub')), parts along dimension 0
- links_fine: int32 [9, 32768], P(None, ('face', 'sub')), may hold values from 0 to 2175, as said below
- sends_fine: int32 [16, 2, 64], P(('face', 'sub')), may hold values from 0 to 2047, as said below
- links_mid: int32 [9, 8192], P(None, ('face', 'sub')), may hold values from 0 to 575, as said below
- sends_mid: int32 [16, 2, 32], P(('face', 'sub')), may hold values from 0 to 511, as said below
- links_coarse: int32 [9, 2048], P(None, ('face', 'sub')), may hold values from 0 to 159, as said below
- sends_coarse: int32 [16, 2, 16], P(('face', 'sub')), may hold values from 0 to 127, as said below
- kernel_enter: bfloat16 [9, 64, 128], replicated, may hold values from -0.25 to 0.25
- gain_enter: float32 [128], replicated, may hold values from 0.5 to 1.5
- shift_enter: float32 [128], replicated, may hold values from -2.5 to 2.5
- kernel_fine: bfloat16 [9, 128, 128], replicated, may hold values from -0.1875 to 0.1875
- gain_fine: float32 [128], replicated, may hold values from 0.5 to 1.5
- shift_fine: float32 [128], replicated, may hold values from -2.5 to 2.5
- kernel_widen: bfloat16 [9, 128, 256], replicated, may hold values from -0.1875 to 0.1875
- gain_widen: float32 [256], replicated, may hold values from 0.5 to 1.5
- shift_widen: float32 [256], replicated, may hold values from -2.5 to 2.5
- kernel_mid: bfloat16 [9, 256, 256], replicated, may hold values from -0.125 to 0.125
- gain_mid: float32 [256], replicated, may hold values from 0.5 to 1.5
- shift_mid: float32 [256], replicated, may hold values from -2.5 to 2.5
- kernel_deep: bfloat16 [9, 256, 512], replicated, may hold values from -0.125 to 0.125
- gain_deep: float32 [512], replicated, may hold values from 0.5 to 1.5
- shift_deep: float32 [512], replicated, may hold values from -2.5 to 2.5
Outputs:
- skip_fine: bfloat16 [65536, 128], P(('groups', 'face', 'sub')), parts along dimension 0
- skip_mid: bfloat16 [16384, 256], P(('groups', 'face', 'sub')), parts along dimension 0
- bottleneck: bfloat16 [4096, 512], P(('groups', 'face', 'sub')), parts along dimension 0
There are 2 independent parts, one for each index of `groups`. A program takes and returns all parts, laid end to end along the dimension named above; an argument that names none is the same for every part. Nothing has to cross between parts.
Inputs may be any that keep to these rules, and one draw needn't show every extreme that they name: links_fine[0, p] is p's own row within its range; every entry below 2048 is a row of the own range, entries from 2048 on index the padded block's received rows. sends_fine[g, 0] lists range g's first 64 rows in some order, sends_fine[g, 1] its last 64 rows in some order. links_mid[0, p] is p's own row within its range; entries from 512 on index the padded block's received rows. sends_mid[g, 0] lists range g's first 32 rows in some order, sends_mid[g, 1] its last 32 rows in some order. links_coarse[0, p] is p's own row within its range; entries from 128 on index the padded block's received rows. sends_coarse[g, 0] lists range g's first 16 rows in some order, sends_coarse[g, 1] its last 16 rows in some order.
All inputs are finite; a program needn't handle non-finite values.
Results may differ from a plain program's by a relative error of at most 0.011.
Values may be sent and summed in bfloat16 or wider, within the bound.
No kernel may reach another device: no remote copies, remote signals or barrier semaphores. Data moves between devices by JAX's collectives and lax.ppermute only.
A program may use at most 64 MiB of HBM per device.

v0:
```python
import jax
import jax.numpy as jnp
from jax import lax
from jax.sharding import PartitionSpec as P


def shifted(value, axis, steps):
    count = lax.axis_size(axis)
    pairs = [(source, (source + steps) % count) for source in range(count)]
    return lax.ppermute(value, axis, pairs)


def unchanged(vector):
    return vector


def pad_block(feat, sends):
    to_left = feat[sends[0, 0]]
    to_right = feat[sends[0, 1]]
    from_left = shifted(to_right, ("face", "sub"), 1)
    from_right = shifted(to_left, ("face", "sub"), -1)
    return jnp.concatenate([feat, from_left, from_right], axis=0)


def convolve(feat, sends, links, kernel):
    padded = pad_block(feat, sends)
    total = jnp.zeros((feat.shape[0], kernel.shape[2]), jnp.float32)
    for tap in range(9):
        total = total + jnp.dot(padded[links[tap]], kernel[tap], preferred_element_type=jnp.float32)
    return total


def normalize(total, gain, shift, count, spread, pick):
    summed = lax.psum(spread(jnp.sum(total, axis=0)), ("face", "sub"))
    mean = pick(summed) / count
    centered = total - mean
    squared = lax.psum(spread(jnp.sum(centered * centered, axis=0)), ("face", "sub"))
    var = pick(squared) / count
    normed = centered * lax.rsqrt(var + 1e-05) * gain + shift
    return jax.nn.gelu(normed, approximate=False).astype(jnp.bfloat16)


def pooling(act):
    return jnp.mean(act.reshape(-1, 4, act.shape[1]).astype(jnp.float32), axis=1).astype(
        jnp.bfloat16
    )


def sharded_layer(feat, sends, links, kernel, gain, shift):
    total = convolve(feat, sends, links, kernel)
    count = float(total.shape[0] * lax.axis_size("face") * lax.axis_size("sub"))
    return normalize(total, gain, shift, count, unchanged, unchanged)


def per_device(
    features,
    links_fine,
    sends_fine,
    links_mid,
    sends_mid,
    links_coarse,
    sends_coarse,
    kernel_enter,
    gain_enter,
    shift_enter,
    kernel_fine,
    gain_fine,
    shift_fine,
    kernel_widen,
    gain_widen,
    shift_widen,
    kernel_mid,
    gain_mid,
    shift_mid,
    kernel_deep,
    gain_deep,
    shift_deep,
):
    first_fine = sharded_layer(
        features, sends_fine, links_fine, kernel_enter, gain_enter, shift_enter
    )
    skip_fine = sharded_layer(
        first_fine, sends_fine, links_fine, kernel_fine, gain_fine, shift_fine
    )
    pooled_mid = pooling(skip_fine)
    first_mid = sharded_layer(
        pooled_mid, sends_mid, links_mid, kernel_widen, gain_widen, shift_widen
    )
    skip_mid = sharded_layer(first_mid, sends_mid, links_mid, kernel_mid, gain_mid, shift_mid)
    pooled_coarse = pooling(skip_mid)
    bottleneck = sharded_layer(
        pooled_coarse, sends_coarse, links_coarse, kernel_deep, gain_deep, shift_deep
    )
    return (skip_fine, skip_mid, bottleneck)


def solution(mesh):
    return jax.shard_map(
        per_device,
        mesh=mesh,
        in_specs=(
            P(("groups", "face", "sub"), None),
            P(None, ("face", "sub")),
            P(("face", "sub"), None, None),
            P(None, ("face", "sub")),
            P(("face", "sub"), None, None),
            P(None, ("face", "sub")),
            P(("face", "sub"), None, None),
            P(),
            P(),
            P(),
            P(),
            P(),
            P(),
            P(),
            P(),
            P(),
            P(),
            P(),
            P(),
            P(),
            P(),
            P(),
        ),
        out_specs=(
            P(("groups", "face", "sub"), None),
            P(("groups", "face", "sub"), None),
            P(("groups", "face", "sub"), None),
        ),
        check_vma=False,
    )
```

profile of v0, /device:TPU:0, one launch (start us, length us, event | category | flops | bytes accessed | tf_op | source)
XLA Modules:
  0.0 590.2 jit_solution(10003050943090886935)
XLA Ops:
  4.5 5.0 collective-permute-start.1
  14.8 6.2 %gather_fusion.10 = bf16[2048,64]{1,0:T(8,128)(2,1)S(1)} fusion(bf16[2176,64]{1,0:T(8,128)(2,1)S(1)} %pad_maximum_fusion, s32[2048]{0:T(1024)S(1)} %broadcast_clamp_fusion), kind=kCustom, calls=%fused_computation.10 | custom fusion | bytes 532480 | tf_op jit(solution)/shard_map/gather | solution.py:29
  21.0 8.1 %gather_fusion.9 = bf16[2048,64]{1,0:T(8,128)(2,1)} fusion(bf16[2176,64]{1,0:T(8,128)(2,1)S(1)} %pad_maximum_fusion, s32[2048]{0:T(1024)S(1)} %broadcast_clamp_fusion.1), kind=kCustom, calls=%fused_computation.9 | custom fusion | bytes 532480 | tf_op jit(solution)/shard_map/gather | solution.py:29
  30.4 8.1 %gather_fusion.8 = bf16[2048,64]{1,0:T(8,128)(2,1)} fusion(bf16[2176,64]{1,0:T(8,128)(2,1)S(1)} %pad_maximum_fusion, s32[2048]{0:T(1024)S(1)} %broadcast_clamp_fusion.2), kind=kCustom, calls=%fused_computation.8 | custom fusion | bytes 532480 | tf_op jit(solution)/shard_map/gather | solution.py:29
  40.7 8.0 %gather_fusion.7 = bf16[2048,64]{1,0:T(8,128)(2,1)} fusion(bf16[2176,64]{1,0:T(8,128)(2,1)S(1)} %pad_maximum_fusion, s32[2048]{0:T(1024)S(1)} %broadcast_clamp_fusion.3), kind=kCustom, calls=%fused_computation.7 | custom fusion | bytes 532480 | tf_op jit(solution)/shard_map/gather | solution.py:29
  51.1 8.0 %gather_fusion.6 = bf16[2048,64]{1,0:T(8,128)(2,1)} fusion(bf16[2176,64]{1,0:T(8,128)(2,1)S(1)} %pad_maximum_fusion, s32[2048]{0:T(1024)S(1)} %broadcast_clamp_fusion.4), kind=kCustom, calls=%fused_computation.6 | custom fusion | bytes 532480 | tf_op jit(solution)/shard_map/gather | solution.py:29
  61.4 8.0 %gather_fusion.5 = bf16[2048,64]{1,0:T(8,128)(2,1)} fusion(bf16[2176,64]{1,0:T(8,128)(2,1)S(1)} %pad_maximum_fusion, s32[2048]{0:T(1024)S(1)} %broadcast_clamp_fusion.5), kind=kCustom, calls=%fused_computation.5 | custom fusion | bytes 532480 | tf_op jit(solution)/shard_map/gather | solution.py:29
  71.8 8.0 %gather_fusion.4 = bf16[2048,64]{1,0:T(8,128)(2,1)} fusion(bf16[2176,64]{1,0:T(8,128)(2,1)S(1)} %pad_maximum_fusion, s32[2048]{0:T(1024)S(1)} %broadcast_clamp_fusion.6), kind=kCustom, calls=%fused_computation.4 | custom fusion | bytes 532480 | tf_op jit(solution)/shard_map/gather | solution.py:29
  82.1 8.0 %gather_fusion.3 = bf16[2048,64]{1,0:T(8,128)(2,1)} fusion(bf16[2176,64]{1,0:T(8,128)(2,1)S(1)} %pad_maximum_fusion, s32[2048]{0:T(1024)S(1)} %broadcast_clamp_fusion.7), kind=kCustom, calls=%fused_computation.3 | custom fusion | bytes 532480 | tf_op jit(solution)/shard_map/gather | solution.py:29
  92.5 8.0 %gather_fusion.2 = bf16[2048,64]{1,0:T(8,128)(2,1)} fusion(bf16[2176,64]{1,0:T(8,128)(2,1)S(1)} %pad_maximum_fusion, s32[2048]{0:T(1024)S(1)} %broadcast_clamp_fusion.8), kind=kCustom, calls=%fused_computation.2 | custom fusion | bytes 532480 | tf_op jit(solution)/shard_map/gather | solution.py:29
  104.0 30.2 %psum.70 = f32[128]{0:T(128)S(1)} all-reduce(f32[128]{0:T(128)S(1)} %get-tuple-element.36), channel_id=1, replica_groups=mesh['groups'=2,'face'=8,'sub'=2] {'face','sub'}, use_global_device_ids=true, to_apply=%region_1.0 | all-reduce | flops 128 | bytes 1024 | tf_op jit(solution)/shard_map/psum | solution.py:34
  134.5 29.5 %psum.71 = f32[128]{0:T(128)S(1)} all-reduce(f32[128]{0:T(128)S(1)} %multiply_reduce_fusion.1), channel_id=1, replica_groups=mesh['groups'=2,'face'=8,'sub'=2] {'face','sub'}, use_global_device_ids=true, to_apply=%region_3.0 | all-reduce | flops 128 | bytes 1024 | tf_op jit(solution)/shard_map/psum | solution.py:37
  173.7 6.2 %gather_fusion.20 = bf16[2048,128]{1,0:T(8,128)(2,1)S(1)} fusion(bf16[2176,128]{1,0:T(8,128)(2,1)S(1)} %pad_maximum_fusion.1, s32[2048]{0:T(1024)S(1)} %broadcast_clamp_fusion.1), kind=kCustom, calls=%fused_computation.20 | custom fusion | bytes 1056768 | tf_op jit(solution)/shard_map/gather | solution.py:29
  179.9 6.2 %gather_fusion.19 = bf16[2048,128]{1,0:T(8,128)(2,1)S(1)} fusion(bf16[2176,128]{1,0:T(8,128)(2,1)S(1)} %pad_maximum_fusion.1, s32[2048]{0:T(1024)S(1)} %broadcast_clamp_fusion.2), kind=kCustom, calls=%fused_computation.19 | custom fusion | bytes 1056768 | tf_op jit(solution)/shard_map/gather | solution.py:29
  186.1 6.2 %gather_fusion.18 = bf16[2048,128]{1,0:T(8,128)(2,1)S(1)} fusion(bf16[2176,128]{1,0:T(8,128)(2,1)S(1)} %pad_maximum_fusion.1, s32[2048]{0:T(1024)S(1)} %broadcast_clamp_fusion.3), kind=kCustom, calls=%fused_computation.18 | custom fusion | bytes 1056768 | tf_op jit(solution)/shard_map/gather | solution.py:29
  192.3 8.0 %gather_fusion.17 = bf16[2048,128]{1,0:T(8,128)(2,1)} fusion(bf16[2176,128]{1,0:T(8,128)(2,1)S(1)} %pad_maximum_fusion.1, s32[2048]{0:T(1024)S(1)} %broadcast_clamp_fusion.4), kind=kCustom, calls=%fused_computation.17 | custom fusion | bytes 1056768 | tf_op jit(solution)/shard_map/gather | solution.py:29
  200.3 8.0 %gather_fusion.16 = bf16[2048,128]{1,0:T(8,128)(2,1)} fusion(bf16[2176,128]{1,0:T(8,128)(2,1)S(1)} %pad_maximum_fusion.1, s32[2048]{0:T(1024)S(1)} %broadcast_clamp_fusion.5), kind=kCustom, calls=%fused_computation.16 | custom fusion | bytes 1056768 | tf_op jit(solution)/shard_map/gather | solution.py:29
  208.2 8.0 %gather_fusion.15 = bf16[2048,128]{1,0:T(8,128)(2,1)} fusion(bf16[2176,128]{1,0:T(8,128)(2,1)S(1)} %pad_maximum_fusion.1, s32[2048]{0:T(1024)S(1)} %broadcast_clamp_fusion.6), kind=kCustom, calls=%fused_computation.15 | custom fusion | bytes 1056768 | tf_op jit(solution)/shard_map/gather | solution.py:29
  216.2 8.0 %gather_fusion.14 = bf16[2048,128]{1,0:T(8,128)(2,1)} fusion(bf16[2176,128]{1,0:T(8,128)(2,1)S(1)} %pad_maximum_fusion.1, s32[2048]{0:T(1024)S(1)} %broadcast_clamp_fusion.7), kind=kCustom, calls=%fused_computation.14 | custom fusion | bytes 1056768 | tf_op jit(solution)/shard_map/gather | solution.py:29
  224.2 8.0 %gather_fusion.21 = bf16[2048,128]{1,0:T(8,128)(2,1)} fusion(bf16[2176,128]{1,0:T(8,128)(2,1)S(1)} %pad_maximum_fusion.1, s32[2048]{0:T(1024)S(1)} %broadcast_clamp_fusion), kind=kCustom, calls=%fused_computation.21 | custom fusion | bytes 1056768 | tf_op jit(solution)/shard_map/gather | solution.py:29
  232.2 6.2 %gather_fusion.13 = bf16[2048,128]{1,0:T(8,128)(2,1)S(1)} fusion(bf16[2176,128]{1,0:T(8,128)(2,1)S(1)} %pad_maximum_fusion.1, s32[2048]{0:T(1024)S(1)} %broadcast_clamp_fusion.8), kind=kCustom, calls=%fused_computation.13 | custom fusion | bytes 1056768 | tf_op jit(solution)/shard_map/gather | solution.py:29
  245.0 33.9 %psum.72 = f32[128]{0:T(128)S(1)} all-reduce(f32[128]{0:T(128)S(1)} %get-tuple-element.38), channel_id=1, replica_groups=mesh['groups'=2,'face'=8,'sub'=2] {'face','sub'}, use_global_device_ids=true, to_apply=%region_5.0 | all-reduce | flops 128 | bytes 1024 | tf_op jit(solution)/shard_map/psum | solution.py:34
  279.2 29.7 %psum.73 = f32[128]{0:T(128)S(1)} all-reduce(f32[128]{0:T(128)S(1)} %multiply_reduce_fusion), channel_id=1, replica_groups=mesh['groups'=2,'face'=8,'sub'=2] {'face','sub'}, use_global_device_ids=true, to_apply=%region_7.0 | all-reduce | flops 128 | bytes 1024 | tf_op jit(solution)/shard_map/psum | solution.py:37
  313.4 4.5 collective-permute-start.5
  344.0 33.9 %psum.74 = f32[256]{0:T(256)S(1)} all-reduce(f32[256]{0:T(256)S(1)} %get-tuple-element.40), channel_id=1, replica_groups=mesh['groups'=2,'face'=8,'sub'=2] {'face','sub'}, use_global_device_ids=true, to_apply=%region_10.0 | all-reduce | flops 256 | bytes 2048 | tf_op jit(solution)/shard_map/psum | solution.py:34
  378.0 29.5 %psum.75 = f32[256]{0:T(256)S(1)} all-reduce(f32[256]{0:T(256)S(1)} %multiply_reduce_fusion.3), channel_id=1, replica_groups=mesh['groups'=2,'face'=8,'sub'=2] {'face','sub'}, use_global_device_ids=true, to_apply=%region_12.0 | all-reduce | flops 256 | bytes 2048 | tf_op jit(solution)/shard_map/psum | solution.py:37
  410.0 4.4 collective-permute-start.7
  437.3 33.9 %psum.76 = f32[256]{0:T(256)S(1)} all-reduce(f32[256]{0:T(256)S(1)} %get-tuple-element.42), channel_id=1, replica_groups=mesh['groups'=2,'face'=8,'sub'=2] {'face','sub'}, use_global_device_ids=true, to_apply=%region_14.0 | all-reduce | flops 256 | bytes 2048 | tf_op jit(solution)/shard_map/psum | solution.py:34
  471.3 29.5 %psum.77 = f32[256]{0:T(256)S(1)} all-reduce(f32[256]{0:T(256)S(1)} %multiply_reduce_fusion.2), channel_id=1, replica_groups=mesh['groups'=2,'face'=8,'sub'=2] {'face','sub'}, use_global_device_ids=true, to_apply=%region_16.0 | all-reduce | flops 256 | bytes 2048 | tf_op jit(solution)/shard_map/psum | solution.py:37
  504.2 4.7 collective-permute-start.9
  525.5 33.9 %psum.78 = f32[512]{0:T(512)S(1)} all-reduce(f32[512]{0:T(512)S(1)} %get-tuple-element.44), channel_id=1, replica_groups=mesh['groups'=2,'face'=8,'sub'=2] {'face','sub'}, use_global_device_ids=true, to_apply=%region_19.0 | all-reduce | flops 512 | bytes 4096 | tf_op jit(solution)/shard_map/psum | solution.py:34
  559.5 29.5 %psum.79 = f32[512]{0:T(512)S(1)} all-reduce(f32[512]{0:T(512)S(1)} %multiply_reduce_fusion.4), channel_id=1, replica_groups=mesh['groups'=2,'face'=8,'sub'=2] {'face','sub'}, use_global_device_ids=true, to_apply=%region_21.0 | all-reduce | flops 512 | bytes 4096 | tf_op jit(solution)/shard_map/psum | solution.py:37
  (226 shorter events, 121.4 us)
Async XLA Ops:
  0.6 10.4 %copy-start.25 = (s32[1,2,32]{2,1,0:T(2,128)S(1)}, s32[1,2,32]{2,1,0:T(2,128)}, u32[]{:S(2)}) copy-start(s32[1,2,32]{2,1,0:T(2,128)} %param.26) | copy-start | bytes 772
  0.6 10.4 %copy-start.14 = (s32[9,512]{1,0:T(8,128)S(1)}, s32[9,512]{1,0:T(8,128)}, u32[]{:S(2)}) copy-start(s32[9,512]{1,0:T(8,128)} %param.25) | copy-start | bytes 55300
  0.7 10.6 %copy-start.26 = (s32[1,2,16]{2,1,0:T(2,128)S(1)}, s32[1,2,16]{2,1,0:T(2,128)}, u32[]{:S(2)}) copy-start(s32[1,2,16]{2,1,0:T(2,128)} %param.28) | copy-start | bytes 388
  0.7 11.1 %copy-start.15 = (s32[9,128]{1,0:T(8,128)S(1)}, s32[9,128]{1,0:T(8,128)}, u32[]{:S(2)}) copy-start(s32[9,128]{1,0:T(8,128)} %param.27) | copy-start | bytes 13828
  3.3 11.3 %collective-permute-start = (bf16[64,64]{1,0:T(8,128)(2,1)S(1)}, bf16[64,64]{1,0:T(8,128)(2,1)S(1)}, u32[]{:S(2)}, u32[]{:S(2)}) collective-permute-start(bf16[64,64]{1,0:T(8,128)(2,1)S(1)} %gather_fusion), channel_id=1, source_target_pairs={{0,1},{1,2},{2,3},{3,4},{4,5},{5,6},{6,7},{7,8},{8,9},{9,10},{10,1... | collective-permute-start | bytes 24584 | tf_op jit(solution)/shard_map/ppermute | solution.py:10
  4.5 10.2 %collective-permute-start.1 = (bf16[64,64]{1,0:T(8,128)(2,1)S(1)}, bf16[64,64]{1,0:T(8,128)(2,1)S(1)}, u32[]{:S(2)}, u32[]{:S(2)}) collective-permute-start(bf16[64,64]{1,0:T(8,128)(2,1)S(1)} %gather_fusion.1), channel_id=1, source_target_pairs={{0,15},{1,0},{2,1},{3,2},{4,3},{5,4},{6,5},{7,6},{8,7},{9,8},{10,9... | collective-permute-start | bytes 24584 | tf_op jit(solution)/shard_map/ppermute | solution.py:10
  21.0 8.1 %copy-start.13 = (bf16[9,64,128]{2,1,0:T(8,128)(2,1)S(1)}, bf16[9,64,128]{2,1,0:T(8,128)(2,1)}, u32[]{:S(2)}) copy-start(bf16[9,64,128]{2,1,0:T(8,128)(2,1)} %param.29) | copy-start | bytes 442372
  100.5 63.5 %copy-start.27 = (f32[128]{0:T(128)S(1)}, f32[128]{0:T(128)}, u32[]{:S(2)}) copy-start(f32[128]{0:T(128)} %param.31) | copy-start | bytes 1540
  100.5 63.5 %copy-start.28 = (f32[128]{0:T(128)S(1)}, f32[128]{0:T(128)}, u32[]{:S(2)}) copy-start(f32[128]{0:T(128)} %param.30) | copy-start | bytes 1540
  167.7 5.9 %collective-permute-start.2 = (bf16[64,128]{1,0:T(8,128)(2,1)S(1)}, bf16[64,128]{1,0:T(8,128)(2,1)S(1)}, u32[]{:S(2)}, u32[]{:S(2)}) collective-permute-start(bf16[64,128]{1,0:T(8,128)(2,1)S(1)} %gather_fusion.11), channel_id=1, source_target_pairs={{0,1},{1,2},{2,3},{3,4},{4,5},{5,6},{6,7},{7,8},{8,9},{9,10},{10,1... | collective-permute-start | bytes 49160 | tf_op jit(solution)/shard_map/ppermute | solution.py:10
  167.8 5.9 collective-permute-start.3
  232.2 6.2 %copy-start.12 = (bf16[9,128,128]{2,1,0:T(8,128)(2,1)S(1)}, bf16[9,128,128]{2,1,0:T(8,128)(2,1)}, u32[]{:S(2)}) copy-start(bf16[9,128,128]{2,1,0:T(8,128)(2,1)} %param.32) | copy-start | bytes 884740
  244.4 64.5 %copy-start.29 = (f32[128]{0:T(128)S(1)}, f32[128]{0:T(128)}, u32[]{:S(2)}) copy-start(f32[128]{0:T(128)} %param.34) | copy-start | bytes 1540
  244.5 64.4 %copy-start.30 = (f32[128]{0:T(128)S(1)}, f32[128]{0:T(128)}, u32[]{:S(2)}) copy-start(f32[128]{0:T(128)} %param.33) | copy-start | bytes 1540
  308.9 9.0 %copy-start.20 = (s32[16]{0:T(128)S(1)}, s32[16]{0:T(128)}, u32[]{:S(2)}) copy-start(s32[16]{0:T(128)} %get-tuple-element.30) | copy-start | bytes 196
  311.4 9.2 %copy-start.7 = (bf16[2048,128]{1,0:T(8,128)(2,1)}, bf16[2048,128]{1,0:T(8,128)(2,1)S(1)}, u32[]{:S(2)}) copy-start(bf16[2048,128]{1,0:T(8,128)(2,1)S(1)} %fusion.40) | copy-start | bytes 1572868
  312.7 5.8 collective-permute-start.4
  313.4 5.8 collective-permute-start.5
  342.2 65.3 %copy-start.21 = (f32[256]{0:T(256)S(1)}, f32[256]{0:T(256)}, u32[]{:S(2)}) copy-start(f32[256]{0:T(256)} %param.37) | copy-start | bytes 3076
  342.2 65.3 %copy-start.22 = (f32[256]{0:T(256)S(1)}, f32[256]{0:T(256)}, u32[]{:S(2)}) copy-start(f32[256]{0:T(256)} %param.36) | copy-start | bytes 3076
  344.0 70.5 %copy-start.19 = (s32[16]{0:T(128)S(1)}, s32[16]{0:T(128)}, u32[]{:S(2)}) copy-start(s32[16]{0:T(128)} %get-tuple-element.31) | copy-start | bytes 196
  410.0 5.9 %collective-permute-start.6 = (bf16[32,256]{1,0:T(8,128)(2,1)S(1)}, bf16[32,256]{1,0:T(8,128)(2,1)S(1)}, u32[]{:S(2)}, u32[]{:S(2)}) collective-permute-start(bf16[32,256]{1,0:T(8,128)(2,1)S(1)} %gather_fusion.33), channel_id=1, source_target_pairs={{0,1},{1,2},{2,3},{3,4},{4,5},{5,6},{6,7},{7,8},{8,9},{9,10},{10,1... | collective-permute-start | bytes 49160 | tf_op jit(solution)/shard_map/ppermute | solution.py:10
  410.0 5.9 collective-permute-start.7
  436.9 63.9 %copy-start.23 = (f32[256]{0:T(256)S(1)}, f32[256]{0:T(256)}, u32[]{:S(2)}) copy-start(f32[256]{0:T(256)} %param.40) | copy-start | bytes 3076
  436.9 63.9 %copy-start.24 = (f32[256]{0:T(256)S(1)}, f32[256]{0:T(256)}, u32[]{:S(2)}) copy-start(f32[256]{0:T(256)} %param.39) | copy-start | bytes 3076
  500.8 8.1 %copy-start.18 = (s32[128]{0:T(128)S(1)}, s32[128]{0:T(128)}, u32[]{:S(2)}) copy-start(s32[128]{0:T(128)} %get-tuple-element.21) | copy-start | bytes 1540
  502.1 9.2 %copy-start.9 = (bf16[512,256]{1,0:T(8,128)(2,1)}, bf16[512,256]{1,0:T(8,128)(2,1)S(1)}, u32[]{:S(2)}) copy-start(bf16[512,256]{1,0:T(8,128)(2,1)S(1)} %fusion.60) | copy-start | bytes 786436
  502.1 10.2 %copy-start = (bf16[9,256,512]{2,1,0:T(8,128)(2,1)S(1)}, bf16[9,256,512]{2,1,0:T(8,128)(2,1)}, u32[]{:S(2)}) copy-start(bf16[9,256,512]{2,1,0:T(8,128)(2,1)} %param.41) | copy-start | bytes 7077892
  503.4 5.8 collective-permute-start.8
  504.2 6.1 %collective-permute-start.9 = (bf16[16,256]{1,0:T(8,128)(2,1)S(1)}, bf16[16,256]{1,0:T(8,128)(2,1)S(1)}, u32[]{:S(2)}, u32[]{:S(2)}) collective-permute-start(bf16[16,256]{1,0:T(8,128)(2,1)S(1)} %gather_fusion.45), channel_id=1, source_target_pairs={{0,15},{1,0},{2,1},{3,2},{4,3},{5,4},{6,5},{7,6},{8,7},{9,8},{10,9... | collective-permute-start | bytes 24584 | tf_op jit(solution)/shard_map/ppermute | solution.py:10
  524.0 65.0 %copy-start.16 = (f32[512]{0:T(512)S(1)}, f32[512]{0:T(512)}, u32[]{:S(2)}) copy-start(f32[512]{0:T(512)} %param.43) | copy-start | bytes 6148
  524.0 65.0 %copy-start.17 = (f32[512]{0:T(512)S(1)}, f32[512]{0:T(512)}, u32[]{:S(2)}) copy-start(f32[512]{0:T(512)} %param.42) | copy-start | bytes 6148
  (9 other events, 10.1 us)
where the time goes:
time: 592 us; the launch traced here: 590 us
  blocking collectives  313 us (53%)
  local copies, waits for them, and re-layouts  188 us (32%)
  matrix products  41.8 us (7%)
  starting transfers between devices  23.9 us (4%)
  other arithmetic  17.6 us (3%)
    gather x45, local copies, waits for them, and re-layouts, convolve(): padded[links[tap]]  175 us
    psum x5, blocking collectives, normalize(): summed = lax.psum(spread(jnp.sum(total, axis=0)), ('face', 'sub'))  166 us
    psum x5, blocking collectives, normalize(): lax.psum(spread(jnp.sum(centered * centered, axis=0)), ('face', 'sub'))  148 us
    dot_general x45, matrix products, convolve(): jnp.dot(padded[links[tap]], kernel[tap], preferred_element_type=jnp.float32)  41.8 us
    ppermute x10, starting transfers between devices, shifted(): return lax.ppermute(value, axis, pairs)  23.9 us
  transfers between devices with their start and end apart: 10, of which 6 were waited for; matrix products, arithmetic and copies ran while one was open for 1% of the time, Pallas kernels for 0%

commit v1 on v0

--- a/solution.py
+++ b/solution.py
@@ -2,6 +2,7 @@
 import jax.numpy as jnp
 from jax import lax
 from jax.sharding import PartitionSpec as P
+from jax.lax import all_gather
 
 
 def shifted(value, axis, steps):
@@ -31,7 +32,8 @@
 
 
 def normalize(total, gain, shift, count, spread, pick):
-    summed = lax.psum(spread(jnp.sum(total, axis=0)), ("face", "sub"))
+    s0 = spread(jnp.sum(total, axis=0))
+    summed = jnp.sum(all_gather(s0, ("face", "sub")), axis=0)
     mean = pick(summed) / count
     centered = total - mean
     squared = lax.psum(spread(jnp.sum(centered * centered, axis=0)), ("face", "sub"))

time: 592 us -> 523 us (0.88)
  blocking collectives: 313 us -> 244 us
    psum x5 -> x0, blocking collectives: 166 us -> none  [normalize(): summed = lax.psum(spread(jnp.sum(total, axis=0)), ('face', 'sub'))]
    all_gather x0 -> x5, blocking collectives: none -> 91.5 us  [normalize(): summed = jnp.sum(all_gather(s0, ('face', 'sub')), axis=0)]
  transfers between devices with their start and end apart: 10 -> 10, of which waited for: 6 -> 6; matrix products, arithmetic and copies ran while one was open for 1% -> 2% of each run, Pallas kernels for 0% -> 0%
where the time goes in v1:
time: 523 us; the launch traced here: 521 us
  blocking collectives  244 us (47%)
  local copies, waits for them, and re-layouts  188 us (36%)
  matrix products  41.8 us (8%)
  starting transfers between devices  23.9 us (5%)
  other arithmetic  17.8 us (3%)
    gather x45, local copies, waits for them, and re-layouts, convolve(): padded[links[tap]]  175 us
    psum x5, blocking collectives, normalize(): lax.psum(spread(jnp.sum(centered * centered, axis=0)), ('face', 'sub'))  153 us
    all_gather x5, blocking collectives, normalize(): summed = jnp.sum(all_gather(s0, ('face', 'sub')), axis=0)  91.5 us
    dot_general x45, matrix products, convolve(): jnp.dot(padded[links[tap]], kernel[tap], preferred_element_type=jnp.float32)  41.8 us
    ppermute x10, starting transfers between devices, shifted(): return lax.ppermute(value, axis, pairs)  23.9 us
  transfers between devices with their start and end apart: 10, of which 6 were waited for; matrix products, arithmetic and copies ran while one was open for 2% of the time, Pallas kernels for 0%

profile of v1, /device:TPU:0, one launch (start us, length us, event | category | flops | bytes accessed | tf_op | source)
XLA Modules:
  0.0 521.1 jit_solution(2677408576819039451)
XLA Ops:
  4.5 5.0 collective-permute-start.1
  14.8 6.2 %gather_fusion.10 = bf16[2048,64]{1,0:T(8,128)(2,1)S(1)} fusion(bf16[2176,64]{1,0:T(8,128)(2,1)S(1)} %pad_maximum_fusion, s32[2048]{0:T(1024)S(1)} %broadcast_clamp_fusion), kind=kCustom, calls=%fused_computation.10 | custom fusion | bytes 532480 | tf_op jit(solution)/shard_map/gather | solution.py:30
  21.0 8.1 %gather_fusion.9 = bf16[2048,64]{1,0:T(8,128)(2,1)} fusion(bf16[2176,64]{1,0:T(8,128)(2,1)S(1)} %pad_maximum_fusion, s32[2048]{0:T(1024)S(1)} %broadcast_clamp_fusion.1), kind=kCustom, calls=%fused_computation.9 | custom fusion | bytes 532480 | tf_op jit(solution)/shard_map/gather | solution.py:30
  30.4 8.1 %gather_fusion.8 = bf16[2048,64]{1,0:T(8,128)(2,1)} fusion(bf16[2176,64]{1,0:T(8,128)(2,1)S(1)} %pad_maximum_fusion, s32[2048]{0:T(1024)S(1)} %broadcast_clamp_fusion.2), kind=kCustom, calls=%fused_computation.8 | custom fusion | bytes 532480 | tf_op jit(solution)/shard_map/gather | solution.py:30
  40.7 8.0 %gather_fusion.7 = bf16[2048,64]{1,0:T(8,128)(2,1)} fusion(bf16[2176,64]{1,0:T(8,128)(2,1)S(1)} %pad_maximum_fusion, s32[2048]{0:T(1024)S(1)} %broadcast_clamp_fusion.3), kind=kCustom, calls=%fused_computation.7 | custom fusion | bytes 532480 | tf_op jit(solution)/shard_map/gather | solution.py:30
  51.1 8.0 %gather_fusion.6 = bf16[2048,64]{1,0:T(8,128)(2,1)} fusion(bf16[2176,64]{1,0:T(8,128)(2,1)S(1)} %pad_maximum_fusion, s32[2048]{0:T(1024)S(1)} %broadcast_clamp_fusion.4), kind=kCustom, calls=%fused_computation.6 | custom fusion | bytes 532480 | tf_op jit(solution)/shard_map/gather | solution.py:30
  61.4 8.0 %gather_fusion.5 = bf16[2048,64]{1,0:T(8,128)(2,1)} fusion(bf16[2176,64]{1,0:T(8,128)(2,1)S(1)} %pad_maximum_fusion, s32[2048]{0:T(1024)S(1)} %broadcast_clamp_fusion.5), kind=kCustom, calls=%fused_computation.5 | custom fusion | bytes 532480 | tf_op jit(solution)/shard_map/gather | solution.py:30
  71.8 8.0 %gather_fusion.4 = bf16[2048,64]{1,0:T(8,128)(2,1)} fusion(bf16[2176,64]{1,0:T(8,128)(2,1)S(1)} %pad_maximum_fusion, s32[2048]{0:T(1024)S(1)} %broadcast_clamp_fusion.6), kind=kCustom, calls=%fused_computation.4 | custom fusion | bytes 532480 | tf_op jit(solution)/shard_map/gather | solution.py:30
  82.1 8.0 %gather_fusion.3 = bf16[2048,64]{1,0:T(8,128)(2,1)} fusion(bf16[2176,64]{1,0:T(8,128)(2,1)S(1)} %pad_maximum_fusion, s32[2048]{0:T(1024)S(1)} %broadcast_clamp_fusion.7), kind=kCustom, calls=%fused_computation.3 | custom fusion | bytes 532480 | tf_op jit(solution)/shard_map/gather | solution.py:30
  92.5 8.0 %gather_fusion.2 = bf16[2048,64]{1,0:T(8,128)(2,1)} fusion(bf16[2176,64]{1,0:T(8,128)(2,1)S(1)} %pad_maximum_fusion, s32[2048]{0:T(1024)S(1)} %broadcast_clamp_fusion.8), kind=kCustom, calls=%fused_computation.2 | custom fusion | bytes 532480 | tf_op jit(solution)/shard_map/gather | solution.py:30
  104.0 19.4 %all-gather.5 = f32[16,1,128]{2,1,0:T(1,128)S(1)} all-gather(f32[1,1,128]{2,1,0:T(1,128)S(1)} %bitcast.333), channel_id=2, replica_groups=mesh['groups'=2,'face'=8,'sub'=2] {'face','sub'}, dimensions={0}, use_global_device_ids=true | all-gather | bytes 8704 | tf_op jit(solution)/shard_map/all_gather | solution.py:36
  123.8 29.8 %psum.35 = f32[128]{0:T(128)S(1)} all-reduce(f32[128]{0:T(128)S(1)} %multiply_reduce_fusion.1), channel_id=1, replica_groups=mesh['groups'=2,'face'=8,'sub'=2] {'face','sub'}, use_global_device_ids=true, to_apply=%region_3.0 | all-reduce | flops 128 | bytes 1024 | tf_op jit(solution)/shard_map/psum | solution.py:39
  163.3 6.2 %gather_fusion.20 = bf16[2048,128]{1,0:T(8,128)(2,1)S(1)} fusion(bf16[2176,128]{1,0:T(8,128)(2,1)S(1)} %pad_maximum_fusion.1, s32[2048]{0:T(1024)S(1)} %broadcast_clamp_fusion.1), kind=kCustom, calls=%fused_computation.20 | custom fusion | bytes 1056768 | tf_op jit(solution)/shard_map/gather | solution.py:30
  169.5 6.2 %gather_fusion.19 = bf16[2048,128]{1,0:T(8,128)(2,1)S(1)} fusion(bf16[2176,128]{1,0:T(8,128)(2,1)S(1)} %pad_maximum_fusion.1, s32[2048]{0:T(1024)S(1)} %broadcast_clamp_fusion.2), kind=kCustom, calls=%fused_computation.19 | custom fusion | bytes 1056768 | tf_op jit(solution)/shard_map/gather | solution.py:30
  175.7 6.2 %gather_fusion.18 = bf16[2048,128]{1,0:T(8,128)(2,1)S(1)} fusion(bf16[2176,128]{1,0:T(8,128)(2,1)S(1)} %pad_maximum_fusion.1, s32[2048]{0:T(1024)S(1)} %broadcast_clamp_fusion.3), kind=kCustom, calls=%fused_computation.18 | custom fusion | bytes 1056768 | tf_op jit(solution)/shard_map/gather | solution.py:30
  181.9 8.0 %gather_fusion.17 = bf16[2048,128]{1,0:T(8,128)(2,1)} fusion(bf16[2176,128]{1,0:T(8,128)(2,1)S(1)} %pad_maximum_fusion.1, s32[2048]{0:T(1024)S(1)} %broadcast_clamp_fusion.4), kind=kCustom, calls=%fused_computation.17 | custom fusion | bytes 1056768 | tf_op jit(solution)/shard_map/gather | solution.py:30
  189.8 8.0 %gather_fusion.16 = bf16[2048,128]{1,0:T(8,128)(2,1)} fusion(bf16[2176,128]{1,0:T(8,128)(2,1)S(1)} %pad_maximum_fusion.1, s32[2048]{0:T(1024)S(1)} %broadcast_clamp_fusion.5), kind=kCustom, calls=%fused_computation.16 | custom fusion | bytes 1056768 | tf_op jit(solution)/shard_map/gather | solution.py:30
  197.8 8.0 %gather_fusion.15 = bf16[2048,128]{1,0:T(8,128)(2,1)} fusion(bf16[2176,128]{1,0:T(8,128)(2,1)S(1)} %pad_maximum_fusion.1, s32[2048]{0:T(1024)S(1)} %broadcast_clamp_fusion.6), kind=kCustom, calls=%fused_computation.15 | custom fusion | bytes 1056768 | tf_op jit(solution)/shard_map/gather | solution.py:30
  205.8 8.0 %gather_fusion.14 = bf16[2048,128]{1,0:T(8,128)(2,1)} fusion(bf16[2176,128]{1,0:T(8,128)(2,1)S(1)} %pad_maximum_fusion.1, s32[2048]{0:T(1024)S(1)} %broadcast_clamp_fusion.7), kind=kCustom, calls=%fused_computation.14 | custom fusion | bytes 1056768 | tf_op jit(solution)/shard_map/gather | solution.py:30
  213.7 8.0 %gather_fusion.21 = bf16[2048,128]{1,0:T(8,128)(2,1)} fusion(bf16[2176,128]{1,0:T(8,128)(2,1)S(1)} %pad_maximum_fusion.1, s32[2048]{0:T(1024)S(1)} %broadcast_clamp_fusion), kind=kCustom, calls=%fused_computation.21 | custom fusion | bytes 1056768 | tf_op jit(solution)/shard_map/gather | solution.py:30
  221.8 6.2 %gather_fusion.13 = bf16[2048,128]{1,0:T(8,128)(2,1)S(1)} fusion(bf16[2176,128]{1,0:T(8,128)(2,1)S(1)} %pad_maximum_fusion.1, s32[2048]{0:T(1024)S(1)} %broadcast_clamp_fusion.8), kind=kCustom, calls=%fused_computation.13 | custom fusion | bytes 1056768 | tf_op jit(solution)/shard_map/gather | solution.py:30
  234.6 18.0 %all-gather.6 = f32[16,1,128]{2,1,0:T(1,128)S(1)} all-gather(f32[1,1,128]{2,1,0:T(1,128)S(1)} %bitcast.334), channel_id=3, replica_groups=mesh['groups'=2,'face'=8,'sub'=2] {'face','sub'}, dimensions={0}, use_global_device_ids=true | all-gather | bytes 8704 | tf_op jit(solution)/shard_map/all_gather | solution.py:36
  252.9 30.8 %psum.36 = f32[128]{0:T(128)S(1)} all-reduce(f32[128]{0:T(128)S(1)} %multiply_reduce_fusion), channel_id=1, replica_groups=mesh['groups'=2,'face'=8,'sub'=2] {'face','sub'}, use_global_device_ids=true, to_apply=%region_7.0 | all-reduce | flops 128 | bytes 1024 | tf_op jit(solution)/shard_map/psum | solution.py:39
  288.2 4.5 collective-permute-start.5
  318.8 18.0 %all-gather.7 = f32[16,1,256]{2,1,0:T(1,128)S(1)} all-gather(f32[1,1,256]{2,1,0:T(1,128)S(1)} %bitcast.331), channel_id=4, replica_groups=mesh['groups'=2,'face'=8,'sub'=2] {'face','sub'}, dimensions={0}, use_global_device_ids=true | all-gather | bytes 17408 | tf_op jit(solution)/shard_map/all_gather | solution.py:36
  337.0 30.7 %psum.37 = f32[256]{0:T(256)S(1)} all-reduce(f32[256]{0:T(256)S(1)} %multiply_reduce_fusion.3), channel_id=1, replica_groups=mesh['groups'=2,'face'=8,'sub'=2] {'face','sub'}, use_global_device_ids=true, to_apply=%region_12.0 | all-reduce | flops 256 | bytes 2048 | tf_op jit(solution)/shard_map/psum | solution.py:39
  370.2 4.4 collective-permute-start.7
  397.5 18.0 %all-gather.8 = f32[16,1,256]{2,1,0:T(1,128)S(1)} all-gather(f32[1,1,256]{2,1,0:T(1,128)S(1)} %bitcast.332), channel_id=5, replica_groups=mesh['groups'=2,'face'=8,'sub'=2] {'face','sub'}, dimensions={0}, use_global_device_ids=true | all-gather | bytes 17408 | tf_op jit(solution)/shard_map/all_gather | solution.py:36
  415.6 30.7 %psum.38 = f32[256]{0:T(256)S(1)} all-reduce(f32[256]{0:T(256)S(1)} %multiply_reduce_fusion.2), channel_id=1, replica_groups=mesh['groups'=2,'face'=8,'sub'=2] {'face','sub'}, use_global_device_ids=true, to_apply=%region_16.0 | all-reduce | flops 256 | bytes 2048 | tf_op jit(solution)/shard_map/psum | solution.py:39
  449.6 4.7 collective-permute-start.9
  471.0 18.0 %all-gather.9 = f32[16,1,512]{2,1,0:T(1,128)S(1)} all-gather(f32[1,1,512]{2,1,0:T(1,128)S(1)} %bitcast.321), channel_id=6, replica_groups=mesh['groups'=2,'face'=8,'sub'=2] {'face','sub'}, dimensions={0}, use_global_device_ids=true | all-gather | bytes 34816 | tf_op jit(solution)/shard_map/all_gather | solution.py:36
  489.1 30.7 %psum.39 = f32[512]{0:T(512)S(1)} all-reduce(f32[512]{0:T(512)S(1)} %multiply_reduce_fusion.4), channel_id=1, replica_groups=mesh['groups'=2,'face'=8,'sub'=2] {'face','sub'}, use_global_device_ids=true, to_apply=%region_21.0 | all-reduce | flops 512 | bytes 4096 | tf_op jit(solution)/shard_map/psum | solution.py:39
  (231 shorter events, 121.6 us)
Async XLA Ops:
  0.6 10.4 %copy-start.25 = (s32[1,2,32]{2,1,0:T(2,128)S(1)}, s32[1,2,32]{2,1,0:T(2,128)}, u32[]{:S(2)}) copy-start(s32[1,2,32]{2,1,0:T(2,128)} %param.26) | copy-start | bytes 772
  0.6 10.4 %copy-start.14 = (s32[9,512]{1,0:T(8,128)S(1)}, s32[9,512]{1,0:T(8,128)}, u32[]{:S(2)}) copy-start(s32[9,512]{1,0:T(8,128)} %param.25) | copy-start | bytes 55300
  0.7 10.6 %copy-start.26 = (s32[1,2,16]{2,1,0:T(2,128)S(1)}, s32[1,2,16]{2,1,0:T(2,128)}, u32[]{:S(2)}) copy-start(s32[1,2,16]{2,1,0:T(2,128)} %param.28) | copy-start | bytes 388
  0.7 11.1 %copy-start.15 = (s32[9,128]{1,0:T(8,128)S(1)}, s32[9,128]{1,0:T(8,128)}, u32[]{:S(2)}) copy-start(s32[9,128]{1,0:T(8,128)} %param.27) | copy-start | bytes 13828
  3.3 11.3 %collective-permute-start = (bf16[64,64]{1,0:T(8,128)(2,1)S(1)}, bf16[64,64]{1,0:T(8,128)(2,1)S(1)}, u32[]{:S(2)}, u32[]{:S(2)}) collective-permute-start(bf16[64,64]{1,0:T(8,128)(2,1)S(1)} %gather_fusion), channel_id=1, source_target_pairs={{0,1},{1,2},{2,3},{3,4},{4,5},{5,6},{6,7},{7,8},{8,9},{9,10},{10,1... | collective-permute-start | bytes 24584 | tf_op jit(solution)/shard_map/ppermute | solution.py:11
  4.5 10.2 %collective-permute-start.1 = (bf16[64,64]{1,0:T(8,128)(2,1)S(1)}, bf16[64,64]{1,0:T(8,128)(2,1)S(1)}, u32[]{:S(2)}, u32[]{:S(2)}) collective-permute-start(bf16[64,64]{1,0:T(8,128)(2,1)S(1)} %gather_fusion.1), channel_id=1, source_target_pairs={{0,15},{1,0},{2,1},{3,2},{4,3},{5,4},{6,5},{7,6},{8,7},{9,8},{10,9... | collective-permute-start | bytes 24584 | tf_op jit(solution)/shard_map/ppermute | solution.py:11
  21.0 8.1 %copy-start.13 = (bf16[9,64,128]{2,1,0:T(8,128)(2,1)S(1)}, bf16[9,64,128]{2,1,0:T(8,128)(2,1)}, u32[]{:S(2)}) copy-start(bf16[9,64,128]{2,1,0:T(8,128)(2,1)} %param.29) | copy-start | bytes 442372
  100.5 53.1 %copy-start.27 = (f32[128]{0:T(128)S(1)}, f32[128]{0:T(128)}, u32[]{:S(2)}) copy-start(f32[128]{0:T(128)} %param.31) | copy-start | bytes 1540
  100.5 53.1 %copy-start.28 = (f32[128]{0:T(128)S(1)}, f32[128]{0:T(128)}, u32[]{:S(2)}) copy-start(f32[128]{0:T(128)} %param.30) | copy-start | bytes 1540
  157.3 5.9 %collective-permute-start.2 = (bf16[64,128]{1,0:T(8,128)(2,1)S(1)}, bf16[64,128]{1,0:T(8,128)(2,1)S(1)}, u32[]{:S(2)}, u32[]{:S(2)}) collective-permute-start(bf16[64,128]{1,0:T(8,128)(2,1)S(1)} %gather_fusion.11), channel_id=1, source_target_pairs={{0,1},{1,2},{2,3},{3,4},{4,5},{5,6},{6,7},{7,8},{8,9},{9,10},{10,1... | collective-permute-start | bytes 49160 | tf_op jit(solution)/shard_map/ppermute | solution.py:11
  157.4 5.9 %collective-permute-start.3 = (bf16[64,128]{1,0:T(8,128)(2,1)S(1)}, bf16[64,128]{1,0:T(8,128)(2,1)S(1)}, u32[]{:S(2)}, u32[]{:S(2)}) collective-permute-start(bf16[64,128]{1,0:T(8,128)(2,1)S(1)} %gather_fusion.12), channel_id=1, source_target_pairs={{0,15},{1,0},{2,1},{3,2},{4,3},{5,4},{6,5},{7,6},{8,7},{9,8},{10,9... | collective-permute-start | bytes 49160 | tf_op jit(solution)/shard_map/ppermute | solution.py:11
  221.8 6.2 %copy-start.12 = (bf16[9,128,128]{2,1,0:T(8,128)(2,1)S(1)}, bf16[9,128,128]{2,1,0:T(8,128)(2,1)}, u32[]{:S(2)}) copy-start(bf16[9,128,128]{2,1,0:T(8,128)(2,1)} %param.32) | copy-start | bytes 884740
  234.0 49.8 %copy-start.29 = (f32[128]{0:T(128)S(1)}, f32[128]{0:T(128)}, u32[]{:S(2)}) copy-start(f32[128]{0:T(128)} %param.34) | copy-start | bytes 1540
  234.0 49.7 %copy-start.30 = (f32[128]{0:T(128)S(1)}, f32[128]{0:T(128)}, u32[]{:S(2)}) copy-start(f32[128]{0:T(128)} %param.33) | copy-start | bytes 1540
  283.8 9.0 %copy-start.20 = (s32[16]{0:T(128)S(1)}, s32[16]{0:T(128)}, u32[]{:S(2)}) copy-start(s32[16]{0:T(128)} %get-tuple-element.30) | copy-start | bytes 196
  286.2 9.2 %copy-start.7 = (bf16[2048,128]{1,0:T(8,128)(2,1)}, bf16[2048,128]{1,0:T(8,128)(2,1)S(1)}, u32[]{:S(2)}) copy-start(bf16[2048,128]{1,0:T(8,128)(2,1)S(1)} %fusion.40) | copy-start | bytes 1572868
  287.6 5.8 %collective-permute-start.4 = (bf16[32,128]{1,0:T(8,128)(2,1)S(1)}, bf16[32,128]{1,0:T(8,128)(2,1)S(1)}, u32[]{:S(2)}, u32[]{:S(2)}) collective-permute-start(bf16[32,128]{1,0:T(8,128)(2,1)S(1)} %gather_fusion.22), channel_id=1, source_target_pairs={{0,1},{1,2},{2,3},{3,4},{4,5},{5,6},{6,7},{7,8},{8,9},{9,10},{10,1... | collective-permute-start | bytes 24584 | tf_op jit(solution)/shard_map/ppermute | solution.py:11
  288.2 5.8 %collective-permute-start.5 = (bf16[32,128]{1,0:T(8,128)(2,1)S(1)}, bf16[32,128]{1,0:T(8,128)(2,1)S(1)}, u32[]{:S(2)}, u32[]{:S(2)}) collective-permute-start(bf16[32,128]{1,0:T(8,128)(2,1)S(1)} %gather_fusion.23), channel_id=1, source_target_pairs={{0,15},{1,0},{2,1},{3,2},{4,3},{5,4},{6,5},{7,6},{8,7},{9,8},{10,9... | collective-permute-start | bytes 24584 | tf_op jit(solution)/shard_map/ppermute | solution.py:11
  317.1 50.6 %copy-start.21 = (f32[256]{0:T(256)S(1)}, f32[256]{0:T(256)}, u32[]{:S(2)}) copy-start(f32[256]{0:T(256)} %param.37) | copy-start | bytes 3076
  317.1 50.6 %copy-start.22 = (f32[256]{0:T(256)S(1)}, f32[256]{0:T(256)}, u32[]{:S(2)}) copy-start(f32[256]{0:T(256)} %param.36) | copy-start | bytes 3076
  318.8 55.8 %copy-start.19 = (s32[16]{0:T(128)S(1)}, s32[16]{0:T(128)}, u32[]{:S(2)}) copy-start(s32[16]{0:T(128)} %get-tuple-element.31) | copy-start | bytes 196
  370.1 5.9 %collective-permute-start.6 = (bf16[32,256]{1,0:T(8,128)(2,1)S(1)}, bf16[32,256]{1,0:T(8,128)(2,1)S(1)}, u32[]{:S(2)}, u32[]{:S(2)}) collective-permute-start(bf16[32,256]{1,0:T(8,128)(2,1)S(1)} %gather_fusion.33), channel_id=1, source_target_pairs={{0,1},{1,2},{2,3},{3,4},{4,5},{5,6},{6,7},{7,8},{8,9},{9,10},{10,1... | collective-permute-start | bytes 49160 | tf_op jit(solution)/shard_map/ppermute | solution.py:11
  370.2 5.9 %collective-permute-start.7 = (bf16[32,256]{1,0:T(8,128)(2,1)S(1)}, bf16[32,256]{1,0:T(8,128)(2,1)S(1)}, u32[]{:S(2)}, u32[]{:S(2)}) collective-permute-start(bf16[32,256]{1,0:T(8,128)(2,1)S(1)} %gather_fusion.34), channel_id=1, source_target_pairs={{0,15},{1,0},{2,1},{3,2},{4,3},{5,4},{6,5},{7,6},{8,7},{9,8},{10,9... | collective-permute-start | bytes 49160 | tf_op jit(solution)/shard_map/ppermute | solution.py:11
  397.1 49.2 %copy-start.23 = (f32[256]{0:T(256)S(1)}, f32[256]{0:T(256)}, u32[]{:S(2)}) copy-start(f32[256]{0:T(256)} %param.40) | copy-start | bytes 3076
  397.1 49.2 %copy-start.24 = (f32[256]{0:T(256)S(1)}, f32[256]{0:T(256)}, u32[]{:S(2)}) copy-start(f32[256]{0:T(256)} %param.39) | copy-start | bytes 3076
  446.3 8.1 %copy-start.18 = (s32[128]{0:T(128)S(1)}, s32[128]{0:T(128)}, u32[]{:S(2)}) copy-start(s32[128]{0:T(128)} %get-tuple-element.21) | copy-start | bytes 1540
  447.5 9.2 %copy-start.9 = (bf16[512,256]{1,0:T(8,128)(2,1)}, bf16[512,256]{1,0:T(8,128)(2,1)S(1)}, u32[]{:S(2)}) copy-start(bf16[512,256]{1,0:T(8,128)(2,1)S(1)} %fusion.60) | copy-start | bytes 786436
  447.5 10.2 %copy-start = (bf16[9,256,512]{2,1,0:T(8,128)(2,1)S(1)}, bf16[9,256,512]{2,1,0:T(8,128)(2,1)}, u32[]{:S(2)}) copy-start(bf16[9,256,512]{2,1,0:T(8,128)(2,1)} %param.41) | copy-start | bytes 7077892
  448.9 5.8 %collective-permute-start.8 = (bf16[16,256]{1,0:T(8,128)(2,1)S(1)}, bf16[16,256]{1,0:T(8,128)(2,1)S(1)}, u32[]{:S(2)}, u32[]{:S(2)}) collective-permute-start(bf16[16,256]{1,0:T(8,128)(2,1)S(1)} %gather_fusion.44), channel_id=1, source_target_pairs={{0,1},{1,2},{2,3},{3,4},{4,5},{5,6},{6,7},{7,8},{8,9},{9,10},{10,1... | collective-permute-start | bytes 24584 | tf_op jit(solution)/shard_map/ppermute | solution.py:11
  449.6 6.1 %collective-permute-start.9 = (bf16[16,256]{1,0:T(8,128)(2,1)S(1)}, bf16[16,256]{1,0:T(8,128)(2,1)S(1)}, u32[]{:S(2)}, u32[]{:S(2)}) collective-permute-start(bf16[16,256]{1,0:T(8,128)(2,1)S(1)} %gather_fusion.45), channel_id=1, source_target_pairs={{0,15},{1,0},{2,1},{3,2},{4,3},{5,4},{6,5},{7,6},{8,7},{9,8},{10,9... | collective-permute-start | bytes 24584 | tf_op jit(solution)/shard_map/ppermute | solution.py:11
  469.4 50.4 %copy-start.16 = (f32[512]{0:T(512)S(1)}, f32[512]{0:T(512)}, u32[]{:S(2)}) copy-start(f32[512]{0:T(512)} %param.43) | copy-start | bytes 6148
  469.4 50.4 %copy-start.17 = (f32[512]{0:T(512)S(1)}, f32[512]{0:T(512)}, u32[]{:S(2)}) copy-start(f32[512]{0:T(512)} %param.42) | copy-start | bytes 6148
  (9 other events, 10.1 us)
